TPU v7x, 32 devices: a whole 2x2x4 slice. The times are simulated.
32 devices in a mesh: lat: 8 (over z, x), ch: 4 (over y, core).
Axes of the slice: x: 2, y: 2, z: 4, core: 2. Of those that a mesh axis runs over, the one named last changes fastest.
Arguments:
- tokens: bfloat16 [1, 16, 8, 69120], P(None, 'lat', 'ch'), may hold values from -6 to 6
- cotangent: bfloat16 [1, 16, 8, 69120], P(None, 'lat', 'ch'), may hold values from -6 to 6
- first_weight: bfloat16 [2, 8, 96, 96], P(None, 'ch'), may hold values from -0.4375 to 0.4375
- first_bias: bfloat16 [2, 8, 96], P(None, 'ch'), may hold values from -6 to 6
- second_weight: bfloat16 [2, 8, 96, 96], P(None, 'ch'), may hold values from -0.4375 to 0.4375
- relu_mask: int32 [1, 2, 8, 256, 1536], P(None, None, 'ch', 'lat'), may hold values 0 or 1
- shrink_mask: int32 [1, 2, 8, 256, 1536], P(None, None, 'ch', 'lat'), may hold values 0 or 1
Outputs:
- token_gradient: bfloat16 [1, 16, 8, 69120], P(None, 'lat', 'ch')
- first_gradient: float32 [2, 8, 96, 96], P(None, 'ch')
- bias_gradient: float32 [2, 8, 96], P(None, 'ch')
- second_gradient: float32 [2, 8, 96, 96], P(None, 'ch')
All inputs are finite; a program needn't handle non-finite values. No bound on the sum of `relu_mask` or of `shrink_mask` on one device may be relied on, other than what follows from the above.
Results may differ from a plain program's by a relative error of at most 0.0093.
Values may be sent and summed in bfloat16 or wider, within the bound.
No kernel may reach another device: no remote copies, remote signals or barrier semaphores. Data moves between devices by JAX's collectives and lax.ppermute only.
A program may use at most 64 MiB of HBM per device.

v0:
```python
import math
import jax
import jax.numpy as jnp
from jax import lax
from jax.sharding import PartitionSpec as P

WAVES = 256


def east_basis(count, waves):
    column = jnp.arange(count, dtype=jnp.int32)[:, None]
    number = jnp.arange(waves, dtype=jnp.int32)[None, :]
    phase = (column * number % count).astype(jnp.float32) * (2.0 * math.pi / count)
    factor = 1.0 / math.sqrt(count)
    return jnp.stack([jnp.cos(phase) * factor, -jnp.sin(phase) * factor], axis=1)


def north_basis(count):
    column = jnp.arange(count, dtype=jnp.int32)[:, None]
    number = jnp.arange(count, dtype=jnp.int32)[None, :]
    phase = (column * number % count).astype(jnp.float32) * (2.0 * math.pi / count)
    factor = 1.0 / math.sqrt(count)
    cosine = jnp.cos(phase) * factor
    sine = jnp.sin(phase) * factor
    upper = jnp.concatenate([cosine, sine], axis=1)
    lower = jnp.concatenate([-sine, cosine], axis=1)
    return jnp.concatenate([upper, lower], axis=0)


def complex_mix(left_real, left_imag, right_real, right_imag, form):
    real_part = jnp.einsum(
        form, left_real, right_real, preferred_element_type=jnp.float32
    ) - jnp.einsum(form, left_imag, right_imag, preferred_element_type=jnp.float32)
    imag_part = jnp.einsum(
        form, left_real, right_imag, preferred_element_type=jnp.float32
    ) + jnp.einsum(form, left_imag, right_real, preferred_element_type=jnp.float32)
    return (real_part, imag_part)


def local(tokens, cotangent, first_weight, first_bias, second_weight, relu_mask, shrink_mask):
    batches, lat_rows, blocks_dev, flat_east = tokens.shape
    block_width = first_weight.shape[2]
    east_cells = flat_east // block_width
    east_table = east_basis(east_cells, WAVES).astype(jnp.bfloat16)

    def to_waves(field):
        grid = field.reshape(batches, lat_rows, blocks_dev, east_cells, block_width)
        return jnp.einsum(
            "bhnwe,wsk->bsnkhe", grid, east_table, preferred_element_type=jnp.float32
        ).astype(jnp.bfloat16)

    spec_tokens = lax.all_to_all(to_waves(tokens), "lat", split_axis=3, concat_axis=4, tiled=True)
    spec_cotangent = lax.all_to_all(
        to_waves(cotangent), "lat", split_axis=3, concat_axis=4, tiled=True
    )
    wave_dev = spec_tokens.shape[3]
    north_cells = spec_tokens.shape[4]
    north_table = (
        north_basis(north_cells).astype(jnp.bfloat16).reshape(2, north_cells, 2, north_cells)
    )
    factor = 1.0 / math.sqrt(north_cells * WAVES)
    shape_modes = (batches, 2, blocks_dev, wave_dev, north_cells, block_width)

    def to_modes(spec):
        return jnp.einsum(
            "tqsp,bsnkpe->btnkqe", north_table, spec, preferred_element_type=jnp.float32
        ).astype(jnp.bfloat16)

    relu_keep = relu_mask.reshape(shape_modes).astype(jnp.float32)
    shrink_keep = shrink_mask.reshape(shape_modes).astype(jnp.bfloat16)
    modes = to_modes(spec_tokens)
    upstream = to_modes(spec_cotangent) * shrink_keep
    before_real, before_imag = complex_mix(
        modes[:, 0], modes[:, 1], first_weight[0], first_weight[1], "bnkqe,nef->bnkqf"
    )
    bias_real = first_bias[0].astype(jnp.float32)[None, :, None, None, :]
    bias_imag = first_bias[1].astype(jnp.float32)[None, :, None, None, :]
    hidden_real = (relu_keep[:, 0] * (before_real + bias_real)).astype(jnp.bfloat16)
    hidden_imag = (relu_keep[:, 1] * (before_imag + bias_imag)).astype(jnp.bfloat16)
    second_real, second_imag = complex_mix(
        hidden_real, -hidden_imag, upstream[:, 0], upstream[:, 1], "bnkqe,bnkqf->nef"
    )
    second_grad = jnp.stack([second_real, second_imag]) * factor
    back_real, back_imag = complex_mix(
        upstream[:, 0], upstream[:, 1], second_weight[0], -second_weight[1], "bnkqf,nef->bnkqe"
    )
    inner_real = (relu_keep[:, 0] * back_real).astype(jnp.bfloat16)
    inner_imag = (relu_keep[:, 1] * back_imag).astype(jnp.bfloat16)
    first_real, first_imag = complex_mix(
        modes[:, 0], -modes[:, 1], inner_real, inner_imag, "bnkqe,bnkqf->nef"
    )
    first_grad = jnp.stack([first_real, first_imag]) * factor
    bias_grad = (
        jnp.stack(
            [
                jnp.sum(inner_real.astype(jnp.float32), axis=(0, 2, 3)),
                jnp.sum(inner_imag.astype(jnp.float32), axis=(0, 2, 3)),
            ]
        )
        * factor
    )
    first_grad, bias_grad, second_grad = lax.psum((first_grad, bias_grad, second_grad), "lat")
    mode_real, mode_imag = complex_mix(
        inner_real, inner_imag, first_weight[0], -first_weight[1], "bnkqf,nef->bnkqe"
    )
    stacked = jnp.stack([mode_real, mode_imag], axis=1).astype(jnp.bfloat16)
    returned = jnp.einsum(
        "tqsp,btnkqe->bsnkpe", north_table, stacked, preferred_element_type=jnp.float32
    ).astype(jnp.bfloat16)
    returned = lax.all_to_all(returned, "lat", split_axis=4, concat_axis=3, tiled=True)
    token_grad = jnp.einsum(
        "bsnkhe,wsk->bhnwe", returned, east_table, preferred_element_type=jnp.float32
    )
    token_grad = token_grad.reshape(batches, lat_rows, blocks_dev, flat_east)
    token_gradient = (token_grad + cotangent.astype(jnp.float32)).astype(jnp.bfloat16)
    return (token_gradient, first_grad, bias_grad, second_grad)


def solution(mesh):
    return jax.shard_map(
        local,
        mesh=mesh,
        in_specs=(
            P(None, "lat", "ch", None),
            P(None, "lat", "ch", None),
            P(None, "ch", None, None),
            P(None, "ch", None),
            P(None, "ch", None, None),
            P(None, None, "ch", "lat", None),
            P(None, None, "ch", "lat", None),
        ),
        out_specs=(
            P(None, "lat", "ch", None),
            P(None, "ch", None, None),
            P(None, "ch", None),
            P(None, "ch", None, None),
        ),
        check_vma=False,
    )
```

profile of v0, /device:TPU:0, one launch (start us, length us, event | category | flops | bytes accessed | tf_op | source)
XLA Modules:
  0.0 157.0 jit_solution(12354883418392423553)
XLA Ops:
  7.2 3.3 %multiply_convert_fusion = (bf16[720,1,256]{2,0,1:T(8,128)(2,1)S(1)}, bf16[720,1,256]{2,0,1:T(8,128)(2,1)S(1)}) fusion(), kind=kLoop, calls=%fused_computation.70 | loop fusion | flops 2580480 | bytes 737280 | tf_op jit(solution)/shard_map/convert.17
  10.5 2.0 %reshape.257 = bf16[2,2,720,96]{3,2,1,0:T(8,128)(2,1)S(1)} reshape(bf16[1,2,2,69120]{3,2,1,0:T(2,128)(2,1)} %param.7) | data formatting | bytes 1105920 | tf_op jit(solution)/shard_map/reshape.34
  12.5 0.5 fusion.26
  13.0 1.2 copy.86
  14.2 7.3 %all-to-all-start.2 = ((bf16[1,2,2,256,2,96]{5,2,4,1,0,3:T(2,128)(2,1)}), bf16[1,2,2,256,2,96]{5,2,4,1,0,3:T(2,128)(2,1)}, u32[]{:S(2)}, u32[]{:S(2)}) async-start(bf16[1,2,2,256,2,96]{5,2,4,1,0,3:T(2,128)(2,1)} %copy.86), calls=%async_computation.2 | async-start | bytes 1048576 | tf_op jit(solution)/shard_map/all_to_all | solution.py:52
  21.4 0.1 negate_convert_fusion
  21.5 0.1 fusion.106
  21.6 0.1 maximum_maximum_fusion
  21.7 0.1 convert_element_type.159
  21.8 0.3 convert_element_type.154
  22.2 0.6 copy-done
  22.8 0.7 reshape.249
  23.5 1.3 fusion.25
  24.8 2.0 %copy.69 = bf16[1,2,2,256,2,96]{5,2,4,1,0,3:T(2,128)(2,1)} copy(bf16[1,2,2,256,2,96]{3,5,2,4,1,0:T(8,128)(2,1)} %fusion.25) | data formatting | bytes 786432 | tf_op jit(solution)/shard_map/convert_element_type | solution.py:50
  26.8 1.2 convert_element_type.163
  28.0 0.4 copy.73
  28.4 0.5 convert_element_type.164
  28.9 0.6 bitcast_convert_fusion.1
  29.5 0.1 fusion.114
  29.6 6.4 %all-to-all-done.2 = bf16[1,2,2,256,2,96]{5,2,4,1,0,3:T(2,128)(2,1)} async-done(((bf16[1,2,2,256,2,96]{5,2,4,1,0,3:T(2,128)(2,1)}), bf16[1,2,2,256,2,96]{5,2,4,1,0,3:T(2,128)(2,1)}, u32[]{:S(2)}, u32[]{:S(2)}) %all-to-all-start.2) | async-done | bytes 393248 | tf_op jit(solution)/shard_map/all_to_all | solution.py:52
  36.0 3.6 %all-to-all-start = ((bf16[1,2,2,256,2,96]{5,2,4,1,0,3:T(2,128)(2,1)}), bf16[1,2,2,256,2,96]{5,2,4,1,0,3:T(2,128)(2,1)S(1)}, u32[]{:S(2)}, u32[]{:S(2)}) async-start(bf16[1,2,2,256,2,96]{5,2,4,1,0,3:T(2,128)(2,1)} %copy.69), calls=%async_computation | async-start | bytes 1048576 | tf_op jit(solution)/shard_map/all_to_all | solution.py:53
  39.7 1.1 copy.87
  40.8 0.5 copy.88
  41.3 0.3 fusion.3
  41.7 1.0 fusion.53
  42.8 1.0 fusion.55
  43.8 10.5 %all-to-all-done = bf16[1,2,2,256,2,96]{5,2,4,1,0,3:T(2,128)(2,1)S(1)} async-done(((bf16[1,2,2,256,2,96]{5,2,4,1,0,3:T(2,128)(2,1)}), bf16[1,2,2,256,2,96]{5,2,4,1,0,3:T(2,128)(2,1)S(1)}, u32[]{:S(2)}, u32[]{:S(2)}) %all-to-all-start) | async-done | bytes 393248 | tf_op jit(solution)/shard_map/all_to_all | solution.py:53
  54.3 0.1 copy.70
  54.4 0.5 copy.71
  55.0 0.3 fusion.10
  55.4 0.5 copy-done.8
  55.9 0.2 fusion.69
  56.1 0.2 fusion.71
  56.4 0.3 fusion.31
  56.7 0.9 convolution_bitcast_fusion.4
  57.6 0.9 convolution_bitcast_fusion.6
  58.5 0.9 convert_reduce_fusion.1
  59.5 0.2 fusion.78
  59.7 0.2 fusion.80
  59.9 1.0 convert_reduce_fusion
  60.9 0.9 convolution_bitcast_fusion.10
  61.8 0.9 convolution_bitcast_fusion.8
  62.7 0.2 fusion.28
  62.9 0.2 fusion.27
  63.2 0.1 maximum_bitcast_fusion
  63.3 0.3 fusion.4
  63.6 1.3 copy.81
  65.0 3.7 %all-to-all-start.1 = ((bf16[1,2,2,32,16,96]{5,1,3,2,0,4:T(2,128)(2,1)}), bf16[1,2,2,32,16,96]{5,1,3,2,0,4:T(2,128)(2,1)S(1)}, u32[]{:S(2)}, u32[]{:S(2)}) async-start(bf16[1,2,2,32,16,96]{5,1,3,2,0,4:T(2,128)(2,1)} %copy.81), calls=%async_computation.1 | async-start | bytes 1048576 | tf_op jit(solution)/shard_map/all_to_all | solution.py:110
  68.7 1.4 fusion.29
  70.1 0.3 fusion.37
  70.4 0.3 fusion.39
  70.7 0.7 maximum_multiply_fusion.1
  71.4 0.3 fusion.33
  71.7 0.3 fusion.35
  72.0 0.7 maximum_multiply_fusion
  72.7 22.6 %psum.22 = f32[2,2,96]{2,1,0:T(2,128)} all-reduce(f32[2,2,96]{2,1,0:T(2,128)S(1)} %maximum_multiply_fusion.2), channel_id=1, replica_groups=mesh['lat'=8,'ch'=4] {'lat'}, use_global_device_ids=true, to_apply=%region_3.4 | all-reduce | flops 384 | bytes 3072 | tf_op jit(solution)/shard_map/psum | solution.py:102
  95.4 0.1 copy.141
  95.5 0.5 convolution_bitcast_fusion
  96.0 0.5 copy.84
  96.5 1.5 reshape.256
  97.9 1.4 add_convert_fusion
  99.3 47.6 %all-reduce.3.cloned.1.call-done = (f32[2,2,96,96]{3,2,1,0:T(8,128)}, f32[2,2,96,96]{3,2,1,0:T(8,128)}) async-done(((f32[2,2,96,96]{3,2,1,0:T(8,128)}, f32[2,2,96,96]{3,2,1,0:T(8,128)}), (f32[2,2,96,96]{3,2,1,0:T(8,128)}, f32[2,2,96,96]{3,2,1,0:T(8,128)})) %all-reduce.3.cloned.1.call-update) | async-done | bytes 294928 | tf_op jit(solution)/shard_map/psum | solution.py:102
  146.9 1.6 %copy.200 = f32[2,2,96,96]{3,2,1,0:T(8,128)} copy(f32[2,2,96,96]{3,2,1,0:T(8,128)} %get-tuple-element.23) | data formatting | bytes 294912
  148.5 1.6 %copy.201 = f32[2,2,96,96]{3,2,1,0:T(8,128)} copy(f32[2,2,96,96]{3,2,1,0:T(8,128)} %get-tuple-element.25) | data formatting | bytes 294912
  (39 shorter events, 0.3 us)
Async XLA Ops:
  10.5 13.1 %copy-start.3 = (bf16[720,1,256]{2,0,1:T(8,128)(2,1)}, bf16[720,1,256]{2,0,1:T(8,128)(2,1)S(1)}, u32[]{:S(2)}) copy-start(bf16[720,1,256]{2,0,1:T(8,128)(2,1)S(1)} %get-tuple-element.18) | copy-start | bytes 1105924
  10.5 13.1 %copy-start.5 = (bf16[720,1,256]{2,0,1:T(8,128)(2,1)}, bf16[720,1,256]{2,0,1:T(8,128)(2,1)S(1)}, u32[]{:S(2)}) copy-start(bf16[720,1,256]{2,0,1:T(8,128)(2,1)S(1)} %get-tuple-element.19) | copy-start | bytes 1105924
  13.0 8.8 %copy-start.7 = (s32[1,2,2,32,1536]{4,3,2,1,0:T(8,128)S(1)}, s32[1,2,2,32,1536]{4,3,2,1,0:T(8,128)}, u32[]{:S(2)}) copy-start(s32[1,2,2,32,1536]{4,3,2,1,0:T(8,128)} %param.12) | copy-start | bytes 2359300
  14.2 21.9 %all-to-all-start.2 = ((bf16[1,2,2,256,2,96]{5,2,4,1,0,3:T(2,128)(2,1)}), bf16[1,2,2,256,2,96]{5,2,4,1,0,3:T(2,128)(2,1)}, u32[]{:S(2)}, u32[]{:S(2)}) async-start(bf16[1,2,2,256,2,96]{5,2,4,1,0,3:T(2,128)(2,1)} %copy.86), calls=%async_computation.2 | async-start | bytes 1048576 | tf_op jit(solution)/shard_map/all_to_all | solution.py:52
  21.7 1.1 copy-start
  26.8 2.1 %copy-start.12 = (bf16[2,2,96]{2,1,0:T(2,128)(2,1)S(1)}, bf16[2,2,96]{2,1,0:T(2,128)(2,1)}, u32[]{:S(2)}) copy-start(bf16[2,2,96]{2,1,0:T(2,128)(2,1)} %param.10) | copy-start | bytes 2308
  36.0 18.3 %all-to-all-start = ((bf16[1,2,2,256,2,96]{5,2,4,1,0,3:T(2,128)(2,1)}), bf16[1,2,2,256,2,96]{5,2,4,1,0,3:T(2,128)(2,1)S(1)}, u32[]{:S(2)}, u32[]{:S(2)}) async-start(bf16[1,2,2,256,2,96]{5,2,4,1,0,3:T(2,128)(2,1)} %copy.69), calls=%async_computation | async-start | bytes 1048576 | tf_op jit(solution)/shard_map/all_to_all | solution.py:53
  40.8 1.0 copy-start.2
  55.0 0.9 copy-start.8
  55.3 1.1 copy-start.1
  55.3 1.0 copy-start.9
  65.0 30.4 %all-to-all-start.1 = ((bf16[1,2,2,32,16,96]{5,1,3,2,0,4:T(2,128)(2,1)}), bf16[1,2,2,32,16,96]{5,1,3,2,0,4:T(2,128)(2,1)S(1)}, u32[]{:S(2)}, u32[]{:S(2)}) async-start(bf16[1,2,2,32,16,96]{5,1,3,2,0,4:T(2,128)(2,1)} %copy.81), calls=%async_computation.1 | async-start | bytes 1048576 | tf_op jit(solution)/shard_map/all_to_all | solution.py:110
  68.6 78.3 %all-reduce.3.cloned.1.call-start = ((), (), s32[]{:S(2)}) async-start(), calls=%async_computation.3 | async-start | bytes 786432 | tf_op jit(solution)/shard_map/psum | solution.py:102
  68.7 1.4 copy-start.14
  68.7 1.7 %copy-start.13 = (f32[2,96,96]{2,1,0:T(8,128)S(1)}, f32[2,96,96]{2,1,0:T(8,128)}, u32[]{:S(2)}) copy-start(f32[2,96,96]{2,1,0:T(8,128)} %convolution_bitcast_fusion.4) | copy-start | bytes 221188
  68.7 2.7 %copy-start.16 = (f32[2,96,96]{2,1,0:T(8,128)S(1)}, f32[2,96,96]{2,1,0:T(8,128)}, u32[]{:S(2)}) copy-start(f32[2,96,96]{2,1,0:T(8,128)} %convolution_bitcast_fusion.10) | copy-start | bytes 221188
  70.4 1.2 copy-start.15
  71.7 1.0 copy-start.10
  71.7 1.0 copy-start.11
  71.7 23.8 %copy-start.4 = (bf16[720,1,256]{2,0,1:T(8,128)(2,1)S(1)}, bf16[720,1,256]{2,0,1:T(8,128)(2,1)}, u32[]{:S(2)}) copy-start(bf16[720,1,256]{2,0,1:T(8,128)(2,1)} %copy-done.3) | copy-start | bytes 1105924
  71.7 23.8 %copy-start.6 = (bf16[720,1,256]{2,0,1:T(8,128)(2,1)S(1)}, bf16[720,1,256]{2,0,1:T(8,128)(2,1)}, u32[]{:S(2)}) copy-start(bf16[720,1,256]{2,0,1:T(8,128)(2,1)} %copy-done.5) | copy-start | bytes 1105924
Sparse Core Ops, SparseCore 0:
  73.4 73.4 all-reduce.2
where the time goes:
time: 158 us; the launch traced here: 157 us
  waiting for transfers between devices  64.6 us (41%)
  blocking collectives  22.6 us (14%)
  local copies, waits for them, and re-layouts  17.4 us (11%)
  matrix products  15 us (9%)
  starting transfers between devices  14.6 us (9%)
  between operations  14.5 us (9%)
  other arithmetic  8.23 us (5%)
    psum x1, waiting for transfers between devices, local(): lax.psum((first_grad, bias_grad, second_grad), 'lat')  47.6 us
    psum x1, blocking collectives, local(): lax.psum((first_grad, bias_grad, second_grad), 'lat')  22.6 us
    all_to_all x1, waiting for transfers between devices, local(): lax.all_to_all(to_waves(cotangent), 'lat', split_axis=3, concat_axis=4, t...  10.5 us
    all_to_all x1, starting transfers between devices, local(): lax.all_to_all(to_waves(tokens), 'lat', split_axis=3, concat_axis=4, tile...  7.28 us
    all_to_all x1, waiting for transfers between devices, local(): lax.all_to_all(to_waves(tokens), 'lat', split_axis=3, concat_axis=4, tile...  6.44 us
    unnamed x36, local copies, waits for them, and re-layouts  4.46 us
    dot_general x5, matrix products, complex_mix(): jnp.einsum(form, left_imag, right_imag, preferred_element_type=jnp.float32)  4.39 us
    all_to_all x1, starting transfers between devices, local(): lax.all_to_all(returned, 'lat', split_axis=4, concat_axis=3, tiled=True)  3.65 us
  transfers between devices with their start and end apart: 4, of which 3 were waited for; matrix products, arithmetic and copies ran while one was open for 12% of the time, Pallas kernels for 0%

commit v1 on v0

--- a/solution.py
+++ b/solution.py
@@ -5,6 +5,22 @@
 from jax.sharding import PartitionSpec as P
 
 WAVES = 256
+
+
+def exchange_in_pairs(array, axis, split, join):
+    ways, here = (lax.axis_size(axis), lax.axis_index(axis))
+    width = array.shape[split] // ways
+    shape = list(array.shape)
+    shape[split] = width
+    height = shape[join]
+    shape[join] = height * ways
+    full = jnp.zeros(shape, array.dtype)
+    for mask in range(ways):
+        part = lax.dynamic_slice_in_dim(array, (here ^ mask) * width, width, axis=split)
+        if mask:
+            part = lax.ppermute(part, axis, [(d, d ^ mask) for d in range(ways)])
+        full = lax.dynamic_update_slice_in_dim(full, part, (here ^ mask) * height, axis=join)
+    return full
 
 
 def east_basis(count, waves):
@@ -49,7 +65,7 @@
             "bhnwe,wsk->bsnkhe", grid, east_table, preferred_element_type=jnp.float32
         ).astype(jnp.bfloat16)
 
-    spec_tokens = lax.all_to_all(to_waves(tokens), "lat", split_axis=3, concat_axis=4, tiled=True)
+    spec_tokens = exchange_in_pairs(to_waves(tokens), "lat", 3, 4)
     spec_cotangent = lax.all_to_all(
         to_waves(cotangent), "lat", split_axis=3, concat_axis=4, tiled=True
     )

time: 158 us -> 156 us (0.987)
  waiting for transfers between devices: 64.6 us -> 51 us
  local copies, waits for them, and re-layouts: 17.4 us -> 28.5 us
  starting transfers between devices: 14.6 us -> 22.6 us
  matrix products: 15 us -> 9.29 us
  other arithmetic: 8.23 us -> 6.52 us
    ppermute x0 -> x7, starting transfers between devices: none -> 14.2 us  [exchange_in_pairs(): part = lax.ppermute(part, axis, [(d, d ^ mask) for d in range(ways)])]
    all_to_all x1, waiting for transfers between devices: 10.5 us -> 0.01 us  [local(): lax.all_to_all(to_waves(cotangent), 'lat', split_axis=3, concat_axis=4, t...]
    another operation x3 -> x13, local copies, waits for them, and re-layouts: 2.09 us -> 9.94 us
    all_to_all x1 -> x0, starting transfers between devices: 7.28 us -> none  [local(): lax.all_to_all(to_waves(tokens), 'lat', split_axis=3, concat_axis=4, tile...]
    all_to_all x1 -> x0, waiting for transfers between devices: 6.44 us -> none  [local(): lax.all_to_all(to_waves(tokens), 'lat', split_axis=3, concat_axis=4, tile...]
    dynamic_update_slice x0 -> x8, local copies, waits for them, and re-layouts: none -> 5.11 us  [exchange_in_pairs(): lax.dynamic_update_slice_in_dim(full, part, (here ^ mask) * height, axis=...]
    dot_general x5, matrix products: 4.39 us -> 2.14 us  [complex_mix(): jnp.einsum(form, left_imag, right_imag, preferred_element_type=jnp.float32)]
    convert_element_type x2 -> x1, local copies, waits for them, and re-layouts: 3.14 us -> 1.15 us  [to_waves(): return jnp.einsum('bhnwe,wsk->bsnkhe', grid, east_table, preferred_elemen...]
  transfers between devices with their start and end apart: 4 -> 10, of which waited for: 3 -> 2; matrix products, arithmetic and copies ran while one was open for 12% -> 17% of each run, Pallas kernels for 0% -> 0%
where the time goes in v1:
time: 156 us; the launch traced here: 155 us
  waiting for transfers between devices  51 us (33%)
  local copies, waits for them, and re-layouts  28.5 us (18%)
  starting transfers between devices  22.6 us (14%)
  blocking collectives  22.3 us (14%)
  between operations  14.7 us (9%)
  matrix products  9.29 us (6%)
  other arithmetic  6.52 us (4%)
    psum x1, waiting for transfers between devices, local(): lax.psum((first_grad, bias_grad, second_grad), 'lat')  49.4 us
    psum x1, blocking collectives, local(): lax.psum((first_grad, bias_grad, second_grad), 'lat')  22.3 us
    ppermute x7, starting transfers between devices, exchange_in_pairs(): part = lax.ppermute(part, axis, [(d, d ^ mask) for d in range(ways)])  14.2 us
    another operation x13, local copies, waits for them, and re-layouts  9.94 us
    dynamic_update_slice x8, local copies, waits for them, and re-layouts, exchange_in_pairs(): lax.dynamic_update_slice_in_dim(full, part, (here ^ mask) * height, axis=...  5.11 us
    all_to_all x1, starting transfers between devices, local(): lax.all_to_all(to_waves(cotangent), 'lat', split_axis=3, concat_axis=4, t...  4.88 us
    unnamed x30, local copies, waits for them, and re-layouts  4.55 us
    all_to_all x1, starting transfers between devices, local(): lax.all_to_all(returned, 'lat', split_axis=4, concat_axis=3, tiled=True)  3.49 us
  transfers between devices with their start and end apart: 10, of which 2 were waited for; matrix products, arithmetic and copies ran while one was open for 17% of the time, Pallas kernels for 0%

profile of v1, /device:TPU:0, one launch (start us, length us, event | category | flops | bytes accessed | tf_op | source)
XLA Modules:
  0.0 155.0 jit_solution(889561334726101264)
XLA Ops:
  7.2 3.3 %multiply_convert_fusion = (bf16[720,1,256]{2,0,1:T(8,128)(2,1)S(1)}, bf16[720,1,256]{2,0,1:T(8,128)(2,1)S(1)}) fusion(), kind=kLoop, calls=%fused_computation.69 | loop fusion | flops 2580480 | bytes 737280 | tf_op jit(solution)/shard_map/convert.17
  10.5 2.0 %reshape.310 = bf16[2,2,720,96]{3,2,1,0:T(8,128)(2,1)S(1)} reshape(bf16[1,2,2,69120]{3,2,1,0:T(2,128)(2,1)} %param.7) | data formatting | bytes 1105920 | tf_op jit(solution)/shard_map/reshape.34
  12.5 0.5 convolution_convert_fusion
  13.1 1.3 constant_dynamic-slice_fusion
  14.4 0.7 copy.101
  15.1 3.0 %collective-permute-start = (bf16[1,2,2,32,2,96]{5,3,2,4,0,1:T(8,128)(2,1)}, bf16[1,2,2,32,2,96]{5,3,2,4,0,1:T(8,128)(2,1)}, u32[]{:S(2)}, u32[]{:S(2)}) collective-permute-start(bf16[1,2,2,32,2,96]{5,3,2,4,0,1:T(8,128)(2,1)} %bitcast.70), channel_id=1, source_target_pairs={{0,4},{4,0},{8,12},{12,8},{16,20},{20,16},{24,28},{28,24},{1,5},{5... | collective-permute-start | bytes 147464 | tf_op jit(solution)/shard_map/ppermute | solution.py:21
  18.1 0.7 copy.103
  18.8 1.6 %collective-permute-start.1 = (bf16[1,2,2,32,2,96]{5,3,2,4,0,1:T(8,128)(2,1)}, bf16[1,2,2,32,2,96]{5,3,2,4,0,1:T(8,128)(2,1)}, u32[]{:S(2)}, u32[]{:S(2)}) collective-permute-start(bf16[1,2,2,32,2,96]{5,3,2,4,0,1:T(8,128)(2,1)} %bitcast.73), channel_id=1, source_target_pairs={{0,8},{4,12},{8,0},{12,4},{16,24},{20,28},{24,16},{28,20},{1,9},{5... | collective-permute-start | bytes 147464 | tf_op jit(solution)/shard_map/ppermute | solution.py:21
  20.4 0.7 copy.105
  21.1 0.7 copy.107
  21.9 3.0 %collective-permute-start.3 = (bf16[1,2,2,32,2,96]{5,3,2,4,0,1:T(8,128)(2,1)}, bf16[1,2,2,32,2,96]{5,3,2,4,0,1:T(8,128)(2,1)}, u32[]{:S(2)}, u32[]{:S(2)}) collective-permute-start(bf16[1,2,2,32,2,96]{5,3,2,4,0,1:T(8,128)(2,1)} %bitcast.79), channel_id=1, source_target_pairs={{0,16},{4,20},{8,24},{12,28},{16,0},{20,4},{24,8},{28,12},{1,17},{... | collective-permute-start | bytes 147464 | tf_op jit(solution)/shard_map/ppermute | solution.py:21
  24.9 0.7 copy.109
  25.6 1.3 collective-permute-start.4
  26.9 0.7 reshape.302
  27.6 0.5 fusion.25
  28.2 1.2 copy.82
  29.3 4.9 %all-to-all-start = ((bf16[1,2,2,256,2,96]{5,2,4,1,0,3:T(2,128)(2,1)}), bf16[1,2,2,256,2,96]{5,2,4,1,0,3:T(2,128)(2,1)S(1)}, u32[]{:S(2)}, u32[]{:S(2)}) async-start(bf16[1,2,2,256,2,96]{5,2,4,1,0,3:T(2,128)(2,1)} %copy.82), calls=%async_computation | async-start | bytes 1048576 | tf_op jit(solution)/shard_map/all_to_all | solution.py:69
  34.6 0.3 convert_element_type.150
  35.0 0.6 copy-done.13
  35.9 1.7 %copy.111 = bf16[2,32,2,2,96]{4,1,3,2,0:T(8,128)(2,1)} copy(bf16[2,32,2,2,96]{1,4,3,2,0:T(8,128)(2,1)} %get-tuple-element.13) | data formatting | bytes 98304 | tf_op jit(solution)/shard_map/dynamic-slice.14
  37.5 1.0 copy.113
  38.7 1.2 copy.86
  39.8 1.5 convert_element_type.160
  41.4 3.9 %collective-permute-start.5 = (bf16[1,2,2,32,2,96]{5,3,2,4,0,1:T(8,128)(2,1)}, bf16[1,2,2,32,2,96]{5,3,2,4,0,1:T(8,128)(2,1)S(1)}, u32[]{:S(2)}, u32[]{:S(2)}) collective-permute-start(bf16[1,2,2,32,2,96]{5,3,2,4,0,1:T(8,128)(2,1)} %bitcast.85), channel_id=1, source_target_pairs={{0,24},{4,28},{8,16},{12,20},{16,8},{20,12},{24,0},{28,4},{1,25},{... | collective-permute-start | bytes 147464 | tf_op jit(solution)/shard_map/ppermute | solution.py:21
  45.3 1.0 copy_dynamic-update-slice_fusion.6
  46.2 1.5 collective-permute-start.6
  47.8 1.0 copy_dynamic-update-slice_fusion.5
  48.7 1.0 copy_dynamic-update-slice_fusion.4
  49.7 1.0 copy_dynamic-update-slice_fusion.3
  50.7 1.0 copy_dynamic-update-slice_fusion.2
  51.8 1.6 %collective-permute-done.6 = bf16[1,2,2,32,2,96]{5,3,2,4,0,1:T(8,128)(2,1)S(1)} collective-permute-done((bf16[1,2,2,32,2,96]{5,3,2,4,0,1:T(8,128)(2,1)S(1)}, bf16[1,2,2,32,2,96]{5,3,2,4,0,1:T(8,128)(2,1)S(1)}, u32[]{:S(2)}, u32[]{:S(2)}) %collective-permute-start.6) | collective-permute-done | bytes 49184 | tf_op jit(solution)/shard_map/ppermute | solution.py:21
  53.5 0.4 fusion.3
  54.1 1.0 fusion.28
  55.3 1.0 fusion.30
  56.5 0.5 copy.84
  57.0 0.3 fusion.10
  57.4 0.5 copy-done.10
  57.9 0.2 fusion.69
  58.1 0.2 fusion.71
  58.4 0.3 convolution_bitcast_fusion.4
  58.6 0.3 convolution_bitcast_fusion.6
  58.9 0.4 convert_reduce_fusion.1
  59.8 0.4 convert_reduce_fusion
  60.3 0.3 convolution_bitcast_fusion.10
  60.6 0.3 convolution_bitcast_fusion.8
  60.9 0.2 fusion.27
  61.1 0.2 fusion.26
  61.5 0.3 fusion.4
  61.8 1.3 copy.94
  63.2 3.5 %all-to-all-start.1 = ((bf16[1,2,2,32,16,96]{5,1,3,2,0,4:T(2,128)(2,1)}), bf16[1,2,2,32,16,96]{5,1,3,2,0,4:T(2,128)(2,1)S(1)}, u32[]{:S(2)}, u32[]{:S(2)}) async-start(bf16[1,2,2,32,16,96]{5,1,3,2,0,4:T(2,128)(2,1)} %copy.94), calls=%async_computation.1 | async-start | bytes 1048576 | tf_op jit(solution)/shard_map/all_to_all | solution.py:126
  66.7 0.3 fusion.36
  67.0 0.3 fusion.38
  67.3 0.7 maximum_multiply_fusion.1
  68.0 0.3 fusion.32
  68.2 0.3 fusion.34
  68.5 0.7 maximum_multiply_fusion
  69.2 22.3 %psum.22 = f32[2,2,96]{2,1,0:T(2,128)} all-reduce(f32[2,2,96]{2,1,0:T(2,128)S(1)} %maximum_multiply_fusion.2), channel_id=1, replica_groups=mesh['lat'=8,'ch'=4] {'lat'}, use_global_device_ids=true, to_apply=%region_3.4 | all-reduce | flops 384 | bytes 3072 | tf_op jit(solution)/shard_map/psum | solution.py:118
  91.7 0.5 convolution_bitcast_fusion
  92.2 0.5 copy.97
  92.7 1.5 reshape.309
  94.1 1.4 add_convert_fusion
  95.5 49.4 %all-reduce.3.cloned.1.call-done = (f32[2,2,96,96]{3,2,1,0:T(8,128)}, f32[2,2,96,96]{3,2,1,0:T(8,128)}) async-done(((f32[2,2,96,96]{3,2,1,0:T(8,128)}, f32[2,2,96,96]{3,2,1,0:T(8,128)}), (f32[2,2,96,96]{3,2,1,0:T(8,128)}, f32[2,2,96,96]{3,2,1,0:T(8,128)})) %all-reduce.3.cloned.1.call-update) | async-done | bytes 294928 | tf_op jit(solution)/shard_map/psum | solution.py:118
  144.9 1.6 %copy.242 = f32[2,2,96,96]{3,2,1,0:T(8,128)} copy(f32[2,2,96,96]{3,2,1,0:T(8,128)} %get-tuple-element.31) | data formatting | bytes 294912
  146.5 1.6 %copy.243 = f32[2,2,96,96]{3,2,1,0:T(8,128)} copy(f32[2,2,96,96]{3,2,1,0:T(8,128)} %get-tuple-element.33) | data formatting | bytes 294912
  (60 shorter events, 2.6 us)
Async XLA Ops:
  10.5 17.1 %copy-start.4 = (bf16[720,1,256]{2,0,1:T(8,128)(2,1)}, bf16[720,1,256]{2,0,1:T(8,128)(2,1)S(1)}, u32[]{:S(2)}) copy-start(bf16[720,1,256]{2,0,1:T(8,128)(2,1)S(1)} %get-tuple-element.26) | copy-start | bytes 1105924
  10.5 17.1 %copy-start.6 = (bf16[720,1,256]{2,0,1:T(8,128)(2,1)}, bf16[720,1,256]{2,0,1:T(8,128)(2,1)S(1)}, u32[]{:S(2)}) copy-start(bf16[720,1,256]{2,0,1:T(8,128)(2,1)S(1)} %get-tuple-element.27) | copy-start | bytes 1105924
  13.1 13.8 %copy-start = (bf16[1,2,2,69120]{3,2,1,0:T(2,128)(2,1)S(1)}, bf16[1,2,2,69120]{3,2,1,0:T(2,128)(2,1)}, u32[]{:S(2)}) copy-start(bf16[1,2,2,69120]{3,2,1,0:T(2,128)(2,1)} %param.8) | copy-start | bytes 1658884
  15.1 26.2 %collective-permute-start = (bf16[1,2,2,32,2,96]{5,3,2,4,0,1:T(8,128)(2,1)}, bf16[1,2,2,32,2,96]{5,3,2,4,0,1:T(8,128)(2,1)}, u32[]{:S(2)}, u32[]{:S(2)}) collective-permute-start(bf16[1,2,2,32,2,96]{5,3,2,4,0,1:T(8,128)(2,1)} %bitcast.70), channel_id=1, source_target_pairs={{0,4},{4,0},{8,12},{12,8},{16,20},{20,16},{24,28},{28,24},{1,5},{5... | collective-permute-start | bytes 147464 | tf_op jit(solution)/shard_map/ppermute | solution.py:21
  18.8 27.4 %collective-permute-start.1 = (bf16[1,2,2,32,2,96]{5,3,2,4,0,1:T(8,128)(2,1)}, bf16[1,2,2,32,2,96]{5,3,2,4,0,1:T(8,128)(2,1)}, u32[]{:S(2)}, u32[]{:S(2)}) collective-permute-start(bf16[1,2,2,32,2,96]{5,3,2,4,0,1:T(8,128)(2,1)} %bitcast.73), channel_id=1, source_target_pairs={{0,8},{4,12},{8,0},{12,4},{16,24},{20,28},{24,16},{28,20},{1,9},{5... | collective-permute-start | bytes 147464 | tf_op jit(solution)/shard_map/ppermute | solution.py:21
  21.1 27.6 %collective-permute-start.2 = (bf16[1,2,2,32,2,96]{5,3,2,4,0,1:T(8,128)(2,1)}, bf16[1,2,2,32,2,96]{5,3,2,4,0,1:T(8,128)(2,1)}, u32[]{:S(2)}, u32[]{:S(2)}) collective-permute-start(bf16[1,2,2,32,2,96]{5,3,2,4,0,1:T(8,128)(2,1)} %bitcast.76), channel_id=1, source_target_pairs={{0,12},{4,8},{8,4},{12,0},{16,28},{20,24},{24,20},{28,16},{1,13},{... | collective-permute-start | bytes 147464 | tf_op jit(solution)/shard_map/ppermute | solution.py:21
  21.9 27.8 %collective-permute-start.3 = (bf16[1,2,2,32,2,96]{5,3,2,4,0,1:T(8,128)(2,1)}, bf16[1,2,2,32,2,96]{5,3,2,4,0,1:T(8,128)(2,1)}, u32[]{:S(2)}, u32[]{:S(2)}) collective-permute-start(bf16[1,2,2,32,2,96]{5,3,2,4,0,1:T(8,128)(2,1)} %bitcast.79), channel_id=1, source_target_pairs={{0,16},{4,20},{8,24},{12,28},{16,0},{20,4},{24,8},{28,12},{1,17},{... | collective-permute-start | bytes 147464 | tf_op jit(solution)/shard_map/ppermute | solution.py:21
  25.6 25.0 %collective-permute-start.4 = (bf16[1,2,2,32,2,96]{5,3,2,4,0,1:T(8,128)(2,1)}, bf16[1,2,2,32,2,96]{5,3,2,4,0,1:T(8,128)(2,1)}, u32[]{:S(2)}, u32[]{:S(2)}) collective-permute-start(bf16[1,2,2,32,2,96]{5,3,2,4,0,1:T(8,128)(2,1)} %bitcast.82), channel_id=1, source_target_pairs={{0,20},{4,16},{8,28},{12,24},{16,4},{20,0},{24,12},{28,8},{1,21},{... | collective-permute-start | bytes 147464 | tf_op jit(solution)/shard_map/ppermute | solution.py:21
  28.2 6.3 %copy-start.8 = (s32[1,2,2,32,1536]{4,3,2,1,0:T(8,128)S(1)}, s32[1,2,2,32,1536]{4,3,2,1,0:T(8,128)}, u32[]{:S(2)}) copy-start(s32[1,2,2,32,1536]{4,3,2,1,0:T(8,128)} %param.12) | copy-start | bytes 2359300
  29.3 27.1 %all-to-all-start = ((bf16[1,2,2,256,2,96]{5,2,4,1,0,3:T(2,128)(2,1)}), bf16[1,2,2,256,2,96]{5,2,4,1,0,3:T(2,128)(2,1)S(1)}, u32[]{:S(2)}, u32[]{:S(2)}) async-start(bf16[1,2,2,256,2,96]{5,2,4,1,0,3:T(2,128)(2,1)} %copy.82), calls=%async_computation | async-start | bytes 1048576 | tf_op jit(solution)/shard_map/all_to_all | solution.py:69
  34.9 0.7 copy-start.13
  35.6 3.0 %copy-start.9 = (s32[1,2,2,32,1536]{4,3,2,1,0:T(8,128)S(1)}, s32[1,2,2,32,1536]{4,3,2,1,0:T(8,128)}, u32[]{:S(2)}) copy-start(s32[1,2,2,32,1536]{4,3,2,1,0:T(8,128)} %param.13) | copy-start | bytes 2359300
  41.4 10.3 %collective-permute-start.5 = (bf16[1,2,2,32,2,96]{5,3,2,4,0,1:T(8,128)(2,1)}, bf16[1,2,2,32,2,96]{5,3,2,4,0,1:T(8,128)(2,1)S(1)}, u32[]{:S(2)}, u32[]{:S(2)}) collective-permute-start(bf16[1,2,2,32,2,96]{5,3,2,4,0,1:T(8,128)(2,1)} %bitcast.85), channel_id=1, source_target_pairs={{0,24},{4,28},{8,16},{12,20},{16,8},{20,12},{24,0},{28,4},{1,25},{... | collective-permute-start | bytes 147464 | tf_op jit(solution)/shard_map/ppermute | solution.py:21
  46.2 7.7 %copy-start.3 = (bf16[2,2,96,96]{3,2,1,0:T(8,128)(2,1)S(1)}, bf16[2,2,96,96]{3,2,1,0:T(8,128)(2,1)}, u32[]{:S(2)}) copy-start(bf16[2,2,96,96]{3,2,1,0:T(8,128)(2,1)} %param.9) | copy-start | bytes 221188
  46.2 7.1 %collective-permute-start.6 = (bf16[1,2,2,32,2,96]{5,3,2,4,0,1:T(8,128)(2,1)S(1)}, bf16[1,2,2,32,2,96]{5,3,2,4,0,1:T(8,128)(2,1)S(1)}, u32[]{:S(2)}, u32[]{:S(2)}) collective-permute-start(bf16[1,2,2,32,2,96]{5,3,2,4,0,1:T(8,128)(2,1)S(1)} %bitcast.377), channel_id=1, source_target_pairs={{0,28},{4,24},{8,20},{12,16},{16,12},{20,8},{24,4},{28,0},{1,29},{... | collective-permute-start | bytes 147464 | tf_op jit(solution)/shard_map/ppermute | solution.py:21
  53.8 1.3 copy-start.1
  57.0 0.9 copy-start.10
  57.4 1.0 copy-start.12
  59.3 1.0 copy-start.2
  61.5 5.3 %copy-start.11 = (bf16[2,32,16,96]{3,1,2,0:T(8,128)(2,1)S(1)}, bf16[2,32,16,96]{3,1,2,0:T(8,128)(2,1)}, u32[]{:S(2)}) copy-start(bf16[2,32,16,96]{3,1,2,0:T(8,128)(2,1)} %fusion.28) | copy-start | bytes 589828
  63.2 28.4 %all-to-all-start.1 = ((bf16[1,2,2,32,16,96]{5,1,3,2,0,4:T(2,128)(2,1)}), bf16[1,2,2,32,16,96]{5,1,3,2,0,4:T(2,128)(2,1)S(1)}, u32[]{:S(2)}, u32[]{:S(2)}) async-start(bf16[1,2,2,32,16,96]{5,1,3,2,0,4:T(2,128)(2,1)} %copy.94), calls=%async_computation.1 | async-start | bytes 1048576 | tf_op jit(solution)/shard_map/all_to_all | solution.py:126
  66.7 78.2 %all-reduce.3.cloned.1.call-start = ((), (), s32[]{:S(2)}) async-start(), calls=%async_computation.2 | async-start | bytes 786432 | tf_op jit(solution)/shard_map/psum | solution.py:118
  68.2 23.4 %copy-start.5 = (bf16[720,1,256]{2,0,1:T(8,128)(2,1)S(1)}, bf16[720,1,256]{2,0,1:T(8,128)(2,1)}, u32[]{:S(2)}) copy-start(bf16[720,1,256]{2,0,1:T(8,128)(2,1)} %copy-done.4) | copy-start | bytes 1105924
  68.5 23.2 %copy-start.7 = (bf16[720,1,256]{2,0,1:T(8,128)(2,1)S(1)}, bf16[720,1,256]{2,0,1:T(8,128)(2,1)}, u32[]{:S(2)}) copy-start(bf16[720,1,256]{2,0,1:T(8,128)(2,1)} %copy-done.6) | copy-start | bytes 1105924
Sparse Core Ops, SparseCore 0:
  71.5 73.3 all-reduce.2
